TPU v7x, 32 devices: a whole 2x2x4 slice. The times are simulated.
32 devices in a mesh: member: 4 (over x, core), tile: 8 (over z, y).
Axes of the slice: x: 2, y: 2, z: 4, core: 2. Of those that a mesh axis runs over, the one named last changes fastest.
Arguments:
- state: bfloat16 [4, 8, 32, 32, 384], P('member', 'tile'), may hold values from -6 to 6
- cotangent: bfloat16 [4, 8, 32, 32, 384], P('member', 'tile'), may hold values from -6 to 6
- neighbors: int32 [8, 8], replicated, may hold values from -1 to 7, as said below
- kernel: float32 [7, 7, 384], replicated, may hold values from -0.875 to 0.875
- conv_bias: float32 [384], replicated, may hold values from -3 to 3
- norm_gain: float32 [384], replicated, may hold values from 0.25 to 1.75
- norm_shift: float32 [384], replicated, may hold values from -2 to 2
- w_in: bfloat16 [384, 1536], replicated, may hold values from -0.3125 to 0.3125
- bias_in: float32 [1536], replicated, may hold values from -3 to 3
- w_out: bfloat16 [1536, 384], replicated, may hold values from -0.15625 to 0.15625
- bias_out: float32 [384], replicated, may hold values from -3 to 3
- layer_scale: float32 [384], replicated, may hold values from 0.3 to 1
Outputs:
- new_state: bfloat16 [4, 8, 32, 32, 384], P('member', 'tile')
- state_grad: bfloat16 [4, 8, 32, 32, 384], P('member', 'tile')
- grad_w_in: float32 [384, 1536], P(None, 'tile')
- grad_w_out: float32 [1536, 384], P('tile')
- grad_kernel: float32 [7, 7, 384], replicated
- grad_bias_in: float32 [1536], replicated
- grad_channels: float32 [5, 384], replicated
Inputs may be any that keep to these rules, and one draw needn't show every extreme that they name: Land tiles and tiles beyond the band's northern or southern edge are -1; longitude wraps around over 6 columns. If neighbors[t, d] = s then neighbors[s, opposite of d] = t. Wet tiles are numbered column by column, the columns of 2 tiles taken alternately upward and downward, so two neighbouring wet tiles differ in index by at most 3, counted cyclically over all wet tiles.
All inputs are finite; a program needn't handle non-finite values.
Results may differ from a plain program's by a relative error of at most 0.0062.
Values may be sent and summed in bfloat16 or wider, within the bound.
A program may use at most 128 MiB of HBM per device.

v0:
```python
import math
import jax
import jax.numpy as jnp
from jax import lax
from jax.sharding import PartitionSpec as P

REACH = 3
GELU_SCALE = 0.7978845608028654
GELU_CUBIC = 0.044715
EPSILON = 1e-06


def shifted(value, axis, steps):
    count = lax.axis_size(axis)
    pairs = [(source, (source + steps) % count) for source in range(count)]
    return lax.ppermute(value, axis, pairs)


def contract_rows(left, right):
    return lax.dot_general(
        left, right, (((0,), (0,)), ((), ())), preferred_element_type=jnp.float32
    )


def contract_cols(left, right):
    return lax.dot_general(
        left, right, (((1,), (1,)), ((), ())), preferred_element_type=jnp.float32
    )


def framed(center, north, south, east, west, north_east, north_west, south_east, south_west):
    lower = jnp.concatenate([south_west, south, south_east], axis=1)
    middle = jnp.concatenate([west, center, east], axis=1)
    upper = jnp.concatenate([north_west, north, north_east], axis=1)
    return jnp.concatenate([lower, middle, upper], axis=0)


def strips(tile, margin):
    edge = tile.shape[0] - margin
    return (tile[:margin], tile[edge:], tile[:, :margin], tile[:, edge:])


def rim_of(tile, margin):
    width = tile.shape[2]
    return jnp.concatenate([piece.reshape(-1, width) for piece in strips(tile, margin)], axis=0)


def keep(pieces, links, source, fresh):
    match = (links == source) & (links >= 0)
    return [jnp.where(match[way], fresh[way], pieces[way]) for way in range(8)]


def from_rim(pieces, links, source, rim, side, margin):
    width = rim.shape[1]
    length = margin * side
    edge = side - margin
    low_rows = rim[:length].reshape(margin, side, width)
    high_rows = rim[length : 2 * length].reshape(margin, side, width)
    low_cols = rim[2 * length : 3 * length].reshape(side, margin, width)
    high_cols = rim[3 * length :].reshape(side, margin, width)
    fresh = [
        low_rows,
        high_rows,
        low_cols,
        high_cols,
        low_rows[:, :margin],
        low_rows[:, edge:],
        high_rows[:, :margin],
        high_rows[:, edge:],
    ]
    return keep(pieces, links, source, fresh)


def assemble(tile, links, myself, count, margin, which):
    side, width = (tile.shape[0], tile.shape[2])
    offsets = list(range(1, REACH + 1)) + [-step for step in range(1, REACH + 1)]
    rows = jnp.zeros((margin, side, width), tile.dtype)
    cols = jnp.zeros((side, margin, width), tile.dtype)
    tip = jnp.zeros((margin, margin, width), tile.dtype)
    pieces = [rows, rows, cols, cols, tip, tip, tip, tip]
    rim = rim_of(tile, margin)
    for offset in offsets:
        source = (myself - offset) % count
        if which == "state":
            moved = shifted(rim, "tile", offset)
        else:
            moved = shifted(rim, "tile", offset)
        pieces = from_rim(pieces, links, source, moved, side, margin)
    return framed(tile, *pieces)


def depthwise(padded, kernel):
    taps = kernel.shape[0]
    side = padded.shape[0] - taps + 1
    total = jnp.zeros((side, side, padded.shape[2]), jnp.float32)
    for row_off in range(taps):
        for col_off in range(taps):
            total = total + kernel[row_off, col_off] * padded[
                row_off : row_off + side, col_off : col_off + side
            ].astype(jnp.float32)
    return total


def transposed(padded, kernel):
    taps = kernel.shape[0]
    side = padded.shape[0] - taps + 1
    total = jnp.zeros((side, side, padded.shape[2]), jnp.float32)
    for row_off in range(taps):
        for col_off in range(taps):
            row_at = taps - 1 - row_off
            col_at = taps - 1 - col_off
            total = total + kernel[row_off, col_off] * padded[
                row_at : row_at + side, col_at : col_at + side
            ].astype(jnp.float32)
    return total


def kernel_grad(padded, grad_mixed):
    taps = padded.shape[0] - grad_mixed.shape[0] + 1
    side = grad_mixed.shape[0]
    rows = []
    for row_off in range(taps):
        line = []
        for col_off in range(taps):
            window = padded[row_off : row_off + side, col_off : col_off + side].astype(jnp.float32)
            line.append(jnp.sum(window * grad_mixed, axis=(0, 1)))
        rows.append(jnp.stack(line))
    return jnp.stack(rows)


def body(
    state,
    cotangent,
    neighbors,
    kernel,
    conv_bias,
    norm_gain,
    norm_shift,
    w_in,
    bias_in,
    w_out,
    bias_out,
    layer_scale,
):
    center = state[0, 0]
    cot_tile = cotangent[0, 0]
    side, width = (center.shape[0], center.shape[2])
    hidden = w_in.shape[1]
    margin = kernel.shape[0] // 2
    count = lax.axis_size("tile")
    myself = lax.axis_index("tile")
    links = neighbors[myself]
    padded = assemble(center, links, myself, count, margin, "state")
    mixed = (depthwise(padded, kernel) + conv_bias).reshape(side * side, width)
    centered = mixed - jnp.mean(mixed, axis=1, keepdims=True)
    variance = jnp.mean(centered * centered, axis=1, keepdims=True)
    inv_std = lax.rsqrt(variance + EPSILON)
    norm_hat = centered * inv_std
    normed = (norm_hat * norm_gain + norm_shift).astype(jnp.bfloat16)
    pre_act = jnp.dot(normed, w_in, preferred_element_type=jnp.float32) + bias_in
    tanh_value = jnp.tanh(GELU_SCALE * (pre_act + GELU_CUBIC * pre_act * pre_act * pre_act))
    activation = (0.5 * pre_act * (1.0 + tanh_value)).astype(jnp.bfloat16)
    branch = jnp.dot(activation, w_out, preferred_element_type=jnp.float32) + bias_out
    flat_state = center.reshape(side * side, width).astype(jnp.float32)
    new_tile = (flat_state + layer_scale * branch).astype(jnp.bfloat16)
    flat_cot = cot_tile.reshape(side * side, width).astype(jnp.float32)
    grad_branch = layer_scale * flat_cot
    branch_low = grad_branch.astype(jnp.bfloat16)
    grad_wout = contract_rows(activation, branch_low)
    grad_bout = jnp.sum(grad_branch, axis=0)
    grad_gamma = jnp.sum(flat_cot * branch, axis=0)
    grad_act = contract_cols(branch_low, w_out)
    slope = 0.5 * (1.0 + tanh_value) + 0.5 * pre_act * (
        1.0 - tanh_value * tanh_value
    ) * GELU_SCALE * (1.0 + 3.0 * GELU_CUBIC * pre_act * pre_act)
    grad_pre = grad_act * slope
    grad_pre_b = grad_pre.astype(jnp.bfloat16)
    grad_win = contract_rows(normed, grad_pre_b)
    grad_bin = jnp.sum(grad_pre, axis=0)
    grad_normed = contract_cols(grad_pre_b, w_in)
    grad_gain = jnp.sum(grad_normed * norm_hat, axis=0)
    grad_shift = jnp.sum(grad_normed, axis=0)
    scaled = grad_normed * norm_gain
    grad_mixed = inv_std * (
        scaled
        - jnp.mean(scaled, axis=1, keepdims=True)
        - norm_hat * jnp.mean(scaled * norm_hat, axis=1, keepdims=True)
    )
    grad_mixed = grad_mixed.reshape(side, side, width)
    grad_low = grad_mixed.astype(jnp.bfloat16)
    padded_grad = assemble(grad_low, links, myself, count, margin, "grad")
    state_grad = (cot_tile.astype(jnp.float32) + transposed(padded_grad, kernel)).astype(
        jnp.bfloat16
    )
    grad_kern = kernel_grad(padded, grad_mixed)
    grad_conv = jnp.sum(grad_mixed, axis=(0, 1))
    share = hidden // count
    (
        grad_win,
        grad_bin,
        grad_kern,
        grad_conv,
        grad_gain,
        grad_shift,
        grad_wout,
        grad_bout,
        grad_gamma,
    ) = lax.psum(
        (
            grad_win,
            grad_bin,
            grad_kern,
            grad_conv,
            grad_gain,
            grad_shift,
            grad_wout,
            grad_bout,
            grad_gamma,
        ),
        ("member", "tile"),
    )
    win_share = lax.dynamic_slice_in_dim(grad_win, myself * share, share, 1)
    wout_share = lax.dynamic_slice_in_dim(grad_wout, myself * share, share, 0)
    factor = 1.0 / math.sqrt(lax.axis_size("member") * count * side * side)
    channels = jnp.stack([grad_conv, grad_gain, grad_shift, grad_bout, grad_gamma]) * factor
    return (
        new_tile.reshape(1, 1, side, side, width),
        state_grad.reshape(1, 1, side, side, width),
        win_share * factor,
        wout_share * factor,
        grad_kern * factor,
        grad_bin * factor,
        channels,
    )


def solution(mesh):
    in_specs = (
        P("member", "tile", None, None, None),
        P("member", "tile", None, None, None),
        P(),
        P(),
        P(),
        P(),
        P(),
        P(),
        P(),
        P(),
        P(),
        P(),
    )
    out_specs = (
        P("member", "tile", None, None, None),
        P("member", "tile", None, None, None),
        P(None, "tile"),
        P("tile", None),
        P(),
        P(),
        P(),
    )
    return jax.shard_map(body, mesh=mesh, in_specs=in_specs, out_specs=out_specs, check_vma=False)
```

profile of v0, /device:TPU:0, one launch (start us, length us, event | category | flops | bytes accessed | tf_op | source)
XLA Modules:
  0.0 402.6 jit_solution(3308788683173243109)
XLA Ops:
  9.6 5.0 %collective-permute-start = (bf16[384,384]{1,0:T(8,128)(2,1)S(1)}, bf16[384,384]{1,0:T(8,128)(2,1)S(1)}, u32[]{:S(2)}, u32[]{:S(2)}) collective-permute-start(bf16[384,384]{1,0:T(8,128)(2,1)S(1)} %pad_maximum_fusion.4), channel_id=1, source_target_pairs={{0,5},{1,6},{2,7},{3,0},{4,1},{5,2},{6,3},{7,4},{8,13},{9,14},{10,... | collective-permute-start | bytes 884744 | tf_op jit(solution)/shard_map/ppermute | solution.py:16
  24.4 6.2 %collective-permute-start.5 = (bf16[384,384]{1,0:T(8,128)(2,1)S(1)}, bf16[384,384]{1,0:T(8,128)(2,1)S(1)}, u32[]{:S(2)}, u32[]{:S(2)}) collective-permute-start(bf16[384,384]{1,0:T(8,128)(2,1)S(1)} %pad_maximum_fusion.4), channel_id=1, source_target_pairs={{0,1},{1,2},{2,3},{3,4},{4,5},{5,6},{6,7},{7,0},{8,9},{9,10},{10,1... | collective-permute-start | bytes 884744 | tf_op jit(solution)/shard_map/ppermute | solution.py:16
  35.6 17.9 %collective-permute-done.3 = bf16[384,384]{1,0:T(8,128)(2,1)} collective-permute-done((bf16[384,384]{1,0:T(8,128)(2,1)S(1)}, bf16[384,384]{1,0:T(8,128)(2,1)}, u32[]{:S(2)}, u32[]{:S(2)}) %collective-permute-start.3) | collective-permute-done | bytes 294944 | tf_op jit(solution)/shard_map/ppermute | solution.py:16
  53.5 4.8 %fusion.143 = (bf16[96,384]{1,0:T(8,128)(2,1)S(1)}, bf16[96,384]{1,0:T(8,128)(2,1)S(1)}, bf16[96,384]{1,0:T(8,128)(2,1)S(1)}, bf16[96,384]{1,0:T(8,128)(2,1)S(1)...) fusion(bf16[384,384]{1,0:T(8,128)(2,1)S(1)} %collective-permute-done.5, ...), kind=kLoop, calls=%fused_computation.287 | loop fusion | flops 221184 | bytes 1253382 | tf_op jit(solution)/shard_map/jit(_where)/select_n | solution.py:50
  58.4 4.8 %fusion.193 = (bf16[96,384]{1,0:T(8,128)(2,1)S(1)}, bf16[96,384]{1,0:T(8,128)(2,1)S(1)}, bf16[96,384]{1,0:T(8,128)(2,1)S(1)}, bf16[96,384]{1,0:T(8,128)(2,1)S(1)...) fusion(bf16[384,384]{1,0:T(8,128)(2,1)S(1)} %collective-permute, ...), kind=kLoop, calls=%fused_computation.419 | loop fusion | flops 221184 | bytes 1548294 | tf_op jit(solution)/shard_map/slice | solution.py:58
  63.2 3.7 fusion.173
  67.0 3.6 select_select_fusion.2
  70.6 3.9 fusion.168
  74.5 4.0 fusion.183
  78.5 3.7 select_select_fusion.3
  82.2 3.7 fusion.178
  86.3 4.5 %maximum_maximum_fusion = (bf16[35,38,384]{2,1,0:T(8,128)(2,1)S(1)}, bf16[35,38,384]{2,1,0:T(8,128)(2,1)S(1)}) fusion(bf16[32,3,384]{2,1,0:T(4,128)(2,1)S(1)} %reshape.433, bf16[32,32,384]{2,1,0:T(8,128)(2,1)} %bitcast.189, bf16[32,3,384]{2,1,0:T(4,128)(2,1)S(1)} %reshape.431, bf16[3,3,384]{2,1,0:T(4,128)(2,1)S(1)} %fusion.178, ...), kind=kLoop, calls=%fused_computation.235 | loop fusion | flops 12257280 | bytes 3151872 | tf_op jit(solution)/shard_map/concatenate | solution.py:35
  91.3 13.3 %fusion.185 = (f32[32,32]{1,0:T(8,128)S(1)}, f32[32,32,384]{2,1,0:T(8,128)}) fusion(f32[384]{0:T(512)} %param.16, bf16[35,38,384]{2,1,0:T(8,128)(2,1)S(1)} %get-tuple-element.141, f32[384]{0:T(512)S(1)} %copy-done.26, f32[384]{0:T(512)S(1)} %copy-done.28, f32[384]{0:T(512)S(1)} %copy-done.32, f32[384]{0:T(512)S(1)} %copy-done.34, f32[384]{0:T(512)S(1)} %copy-done.36, ...), kind=kLoop, calls=%fused_computation.412 | loop fusion | flops 65272832 | bytes 35617792 | tf_op jit(solution)/shard_map/reduce_sum | solution.py:155
  111.4 3.5 fusion.108
  114.9 6.3 %fusion.200 = (f32[1536]{0:T(1024)}, bf16[1024,1536]{1,0:T(8,128)(2,1)S(1)}) fusion(f32[1024,1536]{1,0:T(8,128)S(1)} %get-tuple-element.233, f32[1536]{0:T(1024)S(1)} %copy-done.109, bf16[1024,384]{1,0:T(8,128)(2,1)S(1)} %get-tuple-element.142, bf16[1536,384]{1,0:T(8,128)(2,1)S(1)} %copy-done.108), kind=kOutput, calls=%fused_computation.426 | convolution fusion | flops 1240988160 | bytes 11415552 | tf_op jit(solution)/shard_map/dot_general | solution.py:26
  123.8 5.8 %fusion.101 = (f32[384]{0:T(512)S(1)}, f32[384]{0:T(512)}, f32[384]{0:T(512)}, f32[384]{0:T(512)}, f32[384]{0:T(512)}, /*index=5*/f32[384]{0:T(512)}, f32[384]{0...) fusion(bf16[35,38,384]{2,1,0:T(8,128)(2,1)S(1)} %get-tuple-elem, ...), kind=kLoop, calls=%fused_computation.202 | loop fusion | flops 23979264 | bytes 18919936 | tf_op jit(solution)/shard_map/reduce_sum | solution.py:126
  130.6 3.6 fusion.83
  134.3 4.4 %fusion.51 = (f32[384]{0:T(512)S(1)}, f32[384]{0:T(512)}, f32[384]{0:T(512)}, f32[384]{0:T(512)}, f32[384]{0:T(512)}, /*index=5*/f32[384]{0:T(512)}, f32[384]{0:...) fusion(bf16[35,38,384]{2,1,0:T(8,128)(2,1)S(1)} %get-tuple-elem, ...), kind=kLoop, calls=%fused_computation.152 | loop fusion | flops 21226752 | bytes 15756288 | tf_op jit(solution)/shard_map/reduce_sum | solution.py:126
  199.3 39.4 %all-reduce = (f32[1536]{0:T(1024)S(1)}, f32[1,384]{1,0:T(1,128)S(1)}, f32[1,384]{1,0:T(1,128)S(1)}, f32[1,384]{1,0:T(1,128)}, f32[1,384]{1,0:T(1,128)}, /*index=5*/f32[1,384]{1,0:T(1,128)}) all-reduce(f32[1536]{0:T(1024)} %get-tuple-element.235, f32[1,384]{1,0:T(1,128)} %stack.274, ...), channel_id=1, replica_groups=mesh['member'=4,'tile'=8] {'member','tile'}, use_global_device_ids=true, to_apply=%region_57.58 | all-reduce | flops 3456 | bytes 27648 | tf_op jit(solution)/shard_map/psum | solution.py:208
  238.7 4.1 %collective-permute-start.9 = (bf16[384,384]{1,0:T(8,128)(2,1)S(1)}, bf16[384,384]{1,0:T(8,128)(2,1)}, u32[]{:S(2)}, u32[]{:S(2)}) collective-permute-start(bf16[384,384]{1,0:T(8,128)(2,1)S(1)} %pad_maximum_fusion.5), channel_id=1, source_target_pairs={{0,3},{1,4},{2,5},{3,6},{4,7},{5,0},{6,1},{7,2},{8,11},{9,12},{10,... | collective-permute-start | bytes 884744 | tf_op jit(solution)/shard_map/ppermute | solution.py:16
  244.7 15.3 %collective-permute-done.9 = bf16[384,384]{1,0:T(8,128)(2,1)} collective-permute-done((bf16[384,384]{1,0:T(8,128)(2,1)S(1)}, bf16[384,384]{1,0:T(8,128)(2,1)}, u32[]{:S(2)}, u32[]{:S(2)}) %collective-permute-start.9) | collective-permute-done | bytes 294944 | tf_op jit(solution)/shard_map/ppermute | solution.py:16
  260.0 4.8 %fusion.192 = (bf16[96,384]{1,0:T(8,128)(2,1)S(1)}, bf16[96,384]{1,0:T(8,128)(2,1)S(1)}, bf16[96,384]{1,0:T(8,128)(2,1)S(1)}, bf16[96,384]{1,0:T(8,128)(2,1)S(1)...) fusion(bf16[384,384]{1,0:T(8,128)(2,1)S(1)} %collective-permute-done.7, ...), kind=kLoop, calls=%fused_computation.418 | loop fusion | flops 221184 | bytes 1253382 | tf_op jit(solution)/shard_map/slice | solution.py:58
  264.8 4.9 %fusion.191 = (bf16[96,384]{1,0:T(8,128)(2,1)S(1)}, bf16[96,384]{1,0:T(8,128)(2,1)S(1)}, bf16[96,384]{1,0:T(8,128)(2,1)S(1)}, bf16[96,384]{1,0:T(8,128)(2,1)S(1)...) fusion(bf16[384,384]{1,0:T(8,128)(2,1)S(1)} %collective-permute, ...), kind=kLoop, calls=%fused_computation.417 | loop fusion | flops 221184 | bytes 1548294 | tf_op jit(solution)/shard_map/slice | solution.py:57
  269.6 4.0 fusion.153
  273.6 3.7 select_select_fusion
  277.3 3.7 fusion.148
  281.0 3.7 fusion.163
  284.7 3.6 select_select_fusion.1
  288.4 3.9 fusion.158
  292.8 3.5 maximum_maximum_fusion.2
  296.7 13.8 %fusion.123 = bf16[1,1,32,32,384]{4,3,2,1,0:T(8,128)(2,1)} fusion(bf16[35,38,384]{2,1,0:T(8,128)(2,1)S(1)} %get-tuple-element.139, f32[384]{0:T(512)S(1)} %copy-done.27, f32[384]{0:T(512)S(1)} %copy-done.29, f32[384]{0:T(512)S(1)} %copy-done.33, f32[384]{0:T(512)S(1)} %copy-done.35, f32[384]{0:T(512)S(1)} %copy-done.37, f32[384]{0:T(512)S(1)} %copy-done.39, ...), kind=kLoop, calls=%fused_computation.259 | loop fusion | flops 65667072 | bytes 35612160 | tf_op jit(solution)/shard_map/reshape | solution.py:228
  310.5 80.3 %all-reduce.4.cloned.1.call-done = (f32[384,1536]{0,1:T(8,128)}, f32[1536,384]{1,0:T(8,128)}, f32[7,7,384]{2,1,0:T(8,128)}) async-done(((f32[384,1536]{0,1:T(8,128)}, f32[1536,384]{1,0:T(8,128)}, f32[7,7,384]{2,1,0:T(8,128)}), (f32[384,1536]{0,1:T(8,128)}, f32[1536,384]{1,0:T(8,128)}, f32[7,7,384]{2,1,0:T(8,128)})) %all-reduce.4.cloned.1.call-update) | async-done | bytes 4793872 | tf_op jit(solution)/shard_map/psum | solution.py:208
  (355 shorter events, 95.2 us)
Async XLA Ops:
  7.2 101.2 %copy-start = (bf16[384,1536]{1,0:T(8,128)(2,1)S(1)}, bf16[384,1536]{1,0:T(8,128)(2,1)}, u32[]{:S(2)}) copy-start(bf16[384,1536]{1,0:T(8,128)(2,1)} %param.19) | copy-start | bytes 3538948
  7.2 17.0 %copy-start.4 = (bf16[1,1,32,32,384]{4,3,2,1,0:T(8,128)(2,1)S(1)}, bf16[1,1,32,32,384]{4,3,2,1,0:T(8,128)(2,1)}, u32[]{:S(2)}) copy-start(bf16[1,1,32,32,384]{4,3,2,1,0:T(8,128)(2,1)} %param.13) | copy-start | bytes 2359300
  7.2 17.0 %copy-start.103 = (f32[384]{0:T(512)S(1)}, f32[384]{0:T(512)}, u32[]{:S(2)}) copy-start(f32[384]{0:T(512)} %param.23) | copy-start | bytes 4612
  7.2 383.6 %all-reduce.4.cloned.1.call-start = ((), (), s32[]{:S(2)}) async-start(), calls=%async_computation | async-start | bytes 9609216 | tf_op jit(solution)/shard_map/psum | solution.py:208
  9.6 14.8 %collective-permute-start = (bf16[384,384]{1,0:T(8,128)(2,1)S(1)}, bf16[384,384]{1,0:T(8,128)(2,1)S(1)}, u32[]{:S(2)}, u32[]{:S(2)}) collective-permute-start(bf16[384,384]{1,0:T(8,128)(2,1)S(1)} %pad_maximum_fusion.4), channel_id=1, source_target_pairs={{0,5},{1,6},{2,7},{3,0},{4,1},{5,2},{6,3},{7,4},{8,13},{9,14},{10,... | collective-permute-start | bytes 884744 | tf_op jit(solution)/shard_map/ppermute | solution.py:16
  14.7 21.0 %collective-permute-start.1 = (bf16[384,384]{1,0:T(8,128)(2,1)S(1)}, bf16[384,384]{1,0:T(8,128)(2,1)S(1)}, u32[]{:S(2)}, u32[]{:S(2)}) collective-permute-start(bf16[384,384]{1,0:T(8,128)(2,1)S(1)} %pad_maximum_fusion.4), channel_id=1, source_target_pairs={{0,6},{1,7},{2,0},{3,1},{4,2},{5,3},{6,4},{7,5},{8,14},{9,15},{10,... | collective-permute-start | bytes 884744 | tf_op jit(solution)/shard_map/ppermute | solution.py:16
  16.0 19.6 %collective-permute-start.2 = (bf16[384,384]{1,0:T(8,128)(2,1)S(1)}, bf16[384,384]{1,0:T(8,128)(2,1)S(1)}, u32[]{:S(2)}, u32[]{:S(2)}) collective-permute-start(bf16[384,384]{1,0:T(8,128)(2,1)S(1)} %pad_maximum_fusion.4), channel_id=1, source_target_pairs={{0,7},{1,0},{2,1},{3,2},{4,3},{5,4},{6,5},{7,6},{8,15},{9,8},{10,9... | collective-permute-start | bytes 884744 | tf_op jit(solution)/shard_map/ppermute | solution.py:16
  16.5 37.0 %collective-permute-start.3 = (bf16[384,384]{1,0:T(8,128)(2,1)S(1)}, bf16[384,384]{1,0:T(8,128)(2,1)}, u32[]{:S(2)}, u32[]{:S(2)}) collective-permute-start(bf16[384,384]{1,0:T(8,128)(2,1)S(1)} %pad_maximum_fusion.4), channel_id=1, source_target_pairs={{0,3},{1,4},{2,5},{3,6},{4,7},{5,0},{6,1},{7,2},{8,11},{9,12},{10,... | collective-permute-start | bytes 884744 | tf_op jit(solution)/shard_map/ppermute | solution.py:16
  18.1 35.4 %collective-permute-start.4 = (bf16[384,384]{1,0:T(8,128)(2,1)S(1)}, bf16[384,384]{1,0:T(8,128)(2,1)}, u32[]{:S(2)}, u32[]{:S(2)}) collective-permute-start(bf16[384,384]{1,0:T(8,128)(2,1)S(1)} %pad_maximum_fusion.4), channel_id=1, source_target_pairs={{0,2},{1,3},{2,4},{3,5},{4,6},{5,7},{6,0},{7,1},{8,10},{9,11},{10,... | collective-permute-start | bytes 884744 | tf_op jit(solution)/shard_map/ppermute | solution.py:16
  24.2 66.6 %copy-start.8 = (f32[384]{0:T(512)}, f32[384]{0:T(512)S(1)}, u32[]{:S(2)}) copy-start(f32[384]{0:T(512)S(1)} %get-tuple-element.111) | copy-start | bytes 4612
  24.2 66.7 %copy-start.10 = (f32[384]{0:T(512)}, f32[384]{0:T(512)S(1)}, u32[]{:S(2)}) copy-start(f32[384]{0:T(512)S(1)} %get-tuple-element.112) | copy-start | bytes 4612
  24.2 66.7 %copy-start.12 = (f32[384]{0:T(512)}, f32[384]{0:T(512)S(1)}, u32[]{:S(2)}) copy-start(f32[384]{0:T(512)S(1)} %get-tuple-element.113) | copy-start | bytes 4612
  24.2 66.7 %copy-start.14 = (f32[384]{0:T(512)}, f32[384]{0:T(512)S(1)}, u32[]{:S(2)}) copy-start(f32[384]{0:T(512)S(1)} %get-tuple-element.114) | copy-start | bytes 4612
  24.4 29.1 %collective-permute-start.5 = (bf16[384,384]{1,0:T(8,128)(2,1)S(1)}, bf16[384,384]{1,0:T(8,128)(2,1)S(1)}, u32[]{:S(2)}, u32[]{:S(2)}) collective-permute-start(bf16[384,384]{1,0:T(8,128)(2,1)S(1)} %pad_maximum_fusion.4), channel_id=1, source_target_pairs={{0,1},{1,2},{2,3},{3,4},{4,5},{5,6},{6,7},{7,0},{8,9},{9,10},{10,1... | collective-permute-start | bytes 884744 | tf_op jit(solution)/shard_map/ppermute | solution.py:16
  145.1 12.7 %copy-start.101 = (f32[384]{0:T(512)S(1)}, f32[384]{0:T(512)}, u32[]{:S(2)}) copy-start(f32[384]{0:T(512)} %get-tuple-element.18) | copy-start | bytes 4612
  145.1 13.3 %copy-start.100 = (f32[384]{0:T(512)S(1)}, f32[384]{0:T(512)}, u32[]{:S(2)}) copy-start(f32[384]{0:T(512)} %get-tuple-element.17) | copy-start | bytes 4612
  145.1 13.9 %copy-start.99 = (f32[384]{0:T(512)S(1)}, f32[384]{0:T(512)}, u32[]{:S(2)}) copy-start(f32[384]{0:T(512)} %get-tuple-element.16) | copy-start | bytes 4612
  145.2 18.2 %copy-start.98 = (f32[384]{0:T(512)S(1)}, f32[384]{0:T(512)}, u32[]{:S(2)}) copy-start(f32[384]{0:T(512)} %get-tuple-element.26) | copy-start | bytes 4612
  145.2 18.8 %copy-start.97 = (f32[384]{0:T(512)S(1)}, f32[384]{0:T(512)}, u32[]{:S(2)}) copy-start(f32[384]{0:T(512)} %get-tuple-element.25) | copy-start | bytes 4612
  145.2 19.4 %copy-start.95 = (f32[384]{0:T(512)S(1)}, f32[384]{0:T(512)}, u32[]{:S(2)}) copy-start(f32[384]{0:T(512)} %get-tuple-element.24) | copy-start | bytes 4612
  145.2 20.0 %copy-start.94 = (f32[384]{0:T(512)S(1)}, f32[384]{0:T(512)}, u32[]{:S(2)}) copy-start(f32[384]{0:T(512)} %get-tuple-element.23) | copy-start | bytes 4612
  145.2 27.8 %copy-start.96 = (f32[384]{0:T(512)S(1)}, f32[384]{0:T(512)}, u32[]{:S(2)}) copy-start(f32[384]{0:T(512)} %get-tuple-element.63) | copy-start | bytes 4612
  145.2 40.3 %copy-start.93 = (f32[384]{0:T(512)S(1)}, f32[384]{0:T(512)}, u32[]{:S(2)}) copy-start(f32[384]{0:T(512)} %get-tuple-element.64) | copy-start | bytes 4612
  145.3 52.6 %copy-start.92 = (f32[384]{0:T(512)S(1)}, f32[384]{0:T(512)}, u32[]{:S(2)}) copy-start(f32[384]{0:T(512)} %get-tuple-element.12) | copy-start | bytes 4612
  145.3 53.2 %copy-start.91 = (f32[384]{0:T(512)S(1)}, f32[384]{0:T(512)}, u32[]{:S(2)}) copy-start(f32[384]{0:T(512)} %get-tuple-element.11) | copy-start | bytes 4612
  145.3 53.2 %copy-start.90 = (f32[384]{0:T(512)S(1)}, f32[384]{0:T(512)}, u32[]{:S(2)}) copy-start(f32[384]{0:T(512)} %get-tuple-element.10) | copy-start | bytes 4612
  145.6 93.0 %collective-permute-start.10 = (bf16[384,384]{1,0:T(8,128)(2,1)S(1)}, bf16[384,384]{1,0:T(8,128)(2,1)S(1)}, u32[]{:S(2)}, u32[]{:S(2)}) collective-permute-start(bf16[384,384]{1,0:T(8,128)(2,1)S(1)} %pad_maximum_fusion.5), channel_id=1, source_target_pairs={{0,2},{1,3},{2,4},{3,5},{4,6},{5,7},{6,0},{7,1},{8,10},{9,11},{10,... | collective-permute-start | bytes 884744 | tf_op jit(solution)/shard_map/ppermute | solution.py:16
  146.2 98.5 %collective-permute-start.11 = (bf16[384,384]{1,0:T(8,128)(2,1)S(1)}, bf16[384,384]{1,0:T(8,128)(2,1)S(1)}, u32[]{:S(2)}, u32[]{:S(2)}) collective-permute-start(bf16[384,384]{1,0:T(8,128)(2,1)S(1)} %pad_maximum_fusion.5), channel_id=1, source_target_pairs={{0,1},{1,2},{2,3},{3,4},{4,5},{5,6},{6,7},{7,0},{8,9},{9,10},{10,1... | collective-permute-start | bytes 884744 | tf_op jit(solution)/shard_map/ppermute | solution.py:16
  148.3 96.4 %collective-permute-start.6 = (bf16[384,384]{1,0:T(8,128)(2,1)S(1)}, bf16[384,384]{1,0:T(8,128)(2,1)S(1)}, u32[]{:S(2)}, u32[]{:S(2)}) collective-permute-start(bf16[384,384]{1,0:T(8,128)(2,1)S(1)} %pad_maximum_fusion.5), channel_id=1, source_target_pairs={{0,5},{1,6},{2,7},{3,0},{4,1},{5,2},{6,3},{7,4},{8,13},{9,14},{10,... | collective-permute-start | bytes 884744 | tf_op jit(solution)/shard_map/ppermute | solution.py:16
  151.0 93.7 %collective-permute-start.7 = (bf16[384,384]{1,0:T(8,128)(2,1)S(1)}, bf16[384,384]{1,0:T(8,128)(2,1)S(1)}, u32[]{:S(2)}, u32[]{:S(2)}) collective-permute-start(bf16[384,384]{1,0:T(8,128)(2,1)S(1)} %pad_maximum_fusion.5), channel_id=1, source_target_pairs={{0,6},{1,7},{2,0},{3,1},{4,2},{5,3},{6,4},{7,5},{8,14},{9,15},{10,... | collective-permute-start | bytes 884744 | tf_op jit(solution)/shard_map/ppermute | solution.py:16
  153.0 91.7 %collective-permute-start.8 = (bf16[384,384]{1,0:T(8,128)(2,1)S(1)}, bf16[384,384]{1,0:T(8,128)(2,1)}, u32[]{:S(2)}, u32[]{:S(2)}) collective-permute-start(bf16[384,384]{1,0:T(8,128)(2,1)S(1)} %pad_maximum_fusion.5), channel_id=1, source_target_pairs={{0,7},{1,0},{2,1},{3,2},{4,3},{5,4},{6,5},{7,6},{8,15},{9,8},{10,9... | collective-permute-start | bytes 884744 | tf_op jit(solution)/shard_map/ppermute | solution.py:16
  238.7 21.3 %collective-permute-start.9 = (bf16[384,384]{1,0:T(8,128)(2,1)S(1)}, bf16[384,384]{1,0:T(8,128)(2,1)}, u32[]{:S(2)}, u32[]{:S(2)}) collective-permute-start(bf16[384,384]{1,0:T(8,128)(2,1)S(1)} %pad_maximum_fusion.5), channel_id=1, source_target_pairs={{0,3},{1,4},{2,5},{3,6},{4,7},{5,0},{6,1},{7,2},{8,11},{9,12},{10,... | collective-permute-start | bytes 884744 | tf_op jit(solution)/shard_map/ppermute | solution.py:16
  (92 other events, 398.7 us)
Sparse Core Ops, SparseCore 0:
  243.5 147.2 all-reduce.3
where the time goes:
time: 405 us; the launch traced here: 403 us
  other arithmetic  125 us (31%)
  waiting for transfers between devices  113 us (28%)
  local copies, waits for them, and re-layouts  58.3 us (14%)
  blocking collectives  39.4 us (10%)
  starting transfers between devices  28.4 us (7%)
  matrix products  21.8 us (5%)
  between operations  15.9 us (4%)
    psum x1, waiting for transfers between devices, body(): lax.psum((grad_win, grad_bin, grad_kern, grad_conv, grad_gain, grad_shift...  80.3 us
    select_n x13, other arithmetic, keep(): return [jnp.where(match[way], fresh[way], pieces[way]) for way in range(8)]  50 us
    another operation x56, local copies, waits for them, and re-layouts, kernel_grad(): rows.append(jnp.stack(line))  40.6 us
    psum x1, blocking collectives, body(): lax.psum((grad_win, grad_bin, grad_kern, grad_conv, grad_gain, grad_shift...  39.4 us
    ppermute x12, waiting for transfers between devices, shifted(): return lax.ppermute(value, axis, pairs)  33.2 us
    ppermute x12, starting transfers between devices, shifted(): return lax.ppermute(value, axis, pairs)  28.3 us
    reduce_sum x3, other arithmetic, kernel_grad(): line.append(jnp.sum(window * grad_mixed, axis=(0, 1)))  13.9 us
    reshape x1, other arithmetic, body(): state_grad.reshape(1, 1, side, side, width)  13.8 us
  transfers between devices with their start and end apart: 13, of which 3 were waited for; matrix products, arithmetic and copies ran while one was open for 26% of the time, Pallas kernels for 0%

commit v1 on v0

--- a/solution.py
+++ b/solution.py
@@ -206,18 +206,21 @@
         grad_bout,
         grad_gamma,
     ) = lax.psum(
-        (
-            grad_win,
-            grad_bin,
-            grad_kern,
-            grad_conv,
-            grad_gain,
-            grad_shift,
-            grad_wout,
-            grad_bout,
-            grad_gamma,
+        lax.psum(
+            (
+                grad_win,
+                grad_bin,
+                grad_kern,
+                grad_conv,
+                grad_gain,
+                grad_shift,
+                grad_wout,
+                grad_bout,
+                grad_gamma,
+            ),
+            "tile",
         ),
-        ("member", "tile"),
+        "member",
     )
     win_share = lax.dynamic_slice_in_dim(grad_win, myself * share, share, 1)
     wout_share = lax.dynamic_slice_in_dim(grad_wout, myself * share, share, 0)

time: 405 us -> 464 us (1.15)
  blocking collectives: 39.4 us -> 98.8 us
  waiting for transfers between devices: 113 us -> 164 us
  local copies, waits for them, and re-layouts: 58.3 us -> 11.5 us
    psum x0 -> x1, waiting for transfers between devices: none -> 80.7 us  [body(): lax.psum(lax.psum((grad_win, grad_bin, grad_kern, grad_conv, grad_gain, g...]
    psum x1, blocking collectives: 39.4 us -> 87.9 us  [body(): lax.psum((grad_win, grad_bin, grad_kern, grad_conv, grad_gain, grad_shift...]
    another operation x56, local copies, waits for them, and re-layouts: 40.6 us -> 0.37 us  [kernel_grad(): rows.append(jnp.stack(line))]
    psum x1, waiting for transfers between devices: 80.3 us -> 44.8 us  [body(): lax.psum((grad_win, grad_bin, grad_kern, grad_conv, grad_gain, grad_shift...]
    psum x0 -> x1, blocking collectives: none -> 10.9 us  [body(): lax.psum(lax.psum((grad_win, grad_bin, grad_kern, grad_conv, grad_gain, g...]
    another operation x6, local copies, waits for them, and re-layouts: 5.53 us -> 0.04 us  [body(): jnp.stack([grad_conv, grad_gain, grad_shift, grad_bout, grad_gamma])]
    ppermute x12, waiting for transfers between devices: 33.2 us -> 38.3 us  [shifted(): return lax.ppermute(value, axis, pairs)]
  transfers between devices with their start and end apart: 13 -> 14, of which waited for: 3 -> 5; matrix products, arithmetic and copies ran while one was open for 26% -> 13% of each run, Pallas kernels for 0% -> 0%
where the time goes in v1:
time: 464 us; the launch traced here: 463 us
  waiting for transfers between devices  164 us (35%)
  other arithmetic  125 us (27%)
  blocking collectives  98.8 us (21%)
  starting transfers between devices  25.7 us (6%)
  matrix products  22 us (5%)
  between operations  15.7 us (3%)
  local copies, waits for them, and re-layouts  11.5 us (2%)
    psum x1, blocking collectives, body(): lax.psum((grad_win, grad_bin, grad_kern, grad_conv, grad_gain, grad_shift...  87.9 us
    psum x1, waiting for transfers between devices, body(): lax.psum(lax.psum((grad_win, grad_bin, grad_kern, grad_conv, grad_gain, g...  80.7 us
    select_n x13, other arithmetic, keep(): return [jnp.where(match[way], fresh[way], pieces[way]) for way in range(8)]  48.7 us
    psum x1, waiting for transfers between devices, body(): lax.psum((grad_win, grad_bin, grad_kern, grad_conv, grad_gain, grad_shift...  44.8 us
    ppermute x12, waiting for transfers between devices, shifted(): return lax.ppermute(value, axis, pairs)  38.3 us
    ppermute x12, starting transfers between devices, shifted(): return lax.ppermute(value, axis, pairs)  25.6 us
    reshape x1, other arithmetic, body(): state_grad.reshape(1, 1, side, side, width)  16.2 us
    reduce_sum x1, other arithmetic, body(): centered = mixed - jnp.mean(mixed, axis=1, keepdims=True)  13.3 us
  transfers between devices with their start and end apart: 14, of which 5 were waited for; matrix products, arithmetic and copies ran while one was open for 13% of the time, Pallas kernels for 0%

profile of v1, /device:TPU:0, one launch (start us, length us, event | category | flops | bytes accessed | tf_op | source)
XLA Modules:
  0.0 462.7 jit_solution(1597442583516971888)
XLA Ops:
  9.6 5.0 %collective-permute-start = (bf16[384,384]{1,0:T(8,128)(2,1)S(1)}, bf16[384,384]{1,0:T(8,128)(2,1)S(1)}, u32[]{:S(2)}, u32[]{:S(2)}) collective-permute-start(bf16[384,384]{1,0:T(8,128)(2,1)S(1)} %pad_maximum_fusion.4), channel_id=1, source_target_pairs={{0,5},{1,6},{2,7},{3,0},{4,1},{5,2},{6,3},{7,4},{8,13},{9,14},{10,... | collective-permute-start | bytes 884744 | tf_op jit(solution)/shard_map/ppermute | solution.py:16
  23.2 7.4 %collective-permute-start.5 = (bf16[384,384]{1,0:T(8,128)(2,1)S(1)}, bf16[384,384]{1,0:T(8,128)(2,1)S(1)}, u32[]{:S(2)}, u32[]{:S(2)}) collective-permute-start(bf16[384,384]{1,0:T(8,128)(2,1)S(1)} %pad_maximum_fusion.4), channel_id=1, source_target_pairs={{0,1},{1,2},{2,3},{3,4},{4,5},{5,6},{6,7},{7,0},{8,9},{9,10},{10,1... | collective-permute-start | bytes 884744 | tf_op jit(solution)/shard_map/ppermute | solution.py:16
  34.7 18.6 %collective-permute-done.3 = bf16[384,384]{1,0:T(8,128)(2,1)S(1)} collective-permute-done((bf16[384,384]{1,0:T(8,128)(2,1)S(1)}, bf16[384,384]{1,0:T(8,128)(2,1)S(1)}, u32[]{:S(2)}, u32[]{:S(2)}) %collective-permute-start.3) | collective-permute-done | bytes 294944 | tf_op jit(solution)/shard_map/ppermute | solution.py:16
  53.4 3.7 fusion.143
  57.1 4.8 %fusion.193 = (bf16[96,384]{1,0:T(8,128)(2,1)S(1)}, bf16[96,384]{1,0:T(8,128)(2,1)S(1)}, bf16[96,384]{1,0:T(8,128)(2,1)S(1)}, bf16[96,384]{1,0:T(8,128)(2,1)S(1)...) fusion(bf16[384,384]{1,0:T(8,128)(2,1)S(1)} %collective-permute, ...), kind=kLoop, calls=%fused_computation.419 | loop fusion | flops 221184 | bytes 1548294 | tf_op jit(solution)/shard_map/slice | solution.py:58
  61.9 3.7 fusion.173
  65.6 3.8 select_select_fusion.2
  69.5 3.8 fusion.168
  73.3 3.6 fusion.183
  77.0 3.7 select_select_fusion.3
  80.7 3.8 fusion.178
  84.9 4.6 maximum_maximum_fusion
  89.9 13.3 %fusion.185 = (f32[32,32]{1,0:T(8,128)S(1)}, f32[32,32,384]{2,1,0:T(8,128)}) fusion(f32[384]{0:T(512)} %param.16, bf16[35,38,384]{2,1,0:T(8,128)(2,1)S(1)} %get-tuple-element.150, f32[384]{0:T(512)S(1)} %copy-done.29, f32[384]{0:T(512)S(1)} %copy-done.30, f32[384]{0:T(512)S(1)} %copy-done.32, f32[384]{0:T(512)S(1)} %copy-done.33, f32[384]{0:T(512)S(1)} %copy-done.34, ...), kind=kLoop, calls=%fused_computation.412 | loop fusion | flops 65272832 | bytes 35617792 | tf_op jit(solution)/shard_map/reduce_sum | solution.py:155
  110.1 3.5 fusion.108
  113.6 6.3 %fusion.200 = (f32[1536]{0:T(1024)}, bf16[1024,1536]{1,0:T(8,128)(2,1)S(1)}) fusion(f32[1024,1536]{1,0:T(8,128)S(1)} %get-tuple-element.242, f32[1536]{0:T(1024)S(1)} %copy-done.70, bf16[1024,384]{1,0:T(8,128)(2,1)S(1)} %get-tuple-element.151, bf16[1536,384]{1,0:T(8,128)(2,1)S(1)} %copy-done.69), kind=kOutput, calls=%fused_computation.426 | convolution fusion | flops 1240988160 | bytes 11415552 | tf_op jit(solution)/shard_map/dot_general | solution.py:26
  122.6 5.2 %fusion.101 = (f32[384]{0:T(512)S(1)}, f32[384]{0:T(512)S(1)}, f32[384]{0:T(512)S(1)}, f32[384]{0:T(512)S(1)}, f32[384]{0:T(512)S(1)}, /*index=5*/f32[384]{0:T(5...) fusion(bf16[35,38,384]{2,1,0:T(8,128)(2,1)S(1)} %get-tuple-elem, ...), kind=kLoop, calls=%fused_computation.202 | loop fusion | flops 23979264 | bytes 18919936 | tf_op jit(solution)/shard_map/reduce_sum | solution.py:126
  131.2 3.8 fusion.51
  153.1 87.9 %all-reduce = (f32[1536]{0:T(1024)S(1)}, f32[384]{0:T(512)S(1)}, f32[384]{0:T(512)S(1)}, f32[384]{0:T(512)S(1)}, f32[384]{0:T(512)S(1)}, /*index=5*/f32[384]{0:T(512)S(1)}) all-reduce(f32[1536]{0:T(1024)S(1)} %copy-done.63, f32[384]{0:T(512)S(1)} %get-tuple-element.62, ...), channel_id=1, replica_groups=mesh['member'=4,'tile'=8] {'tile'}, use_global_device_ids=true, to_apply=%region_60.61 | all-reduce | flops 3456 | bytes 27648 | tf_op jit(solution)/shard_map/psum | solution.py:209
  241.1 10.9 %all-reduce.2 = (f32[1536]{0:T(1024)S(1)}, f32[1,384]{1,0:T(1,128)S(1)}, f32[1,384]{1,0:T(1,128)S(1)}, f32[1,384]{1,0:T(1,128)S(1)}, f32[1,384]{1,0:T(1,128)S(1)}, /*index=5*/f32[1,384]{1,0:T(1,128)S(1)}) all-reduce(f32[1536]{0:T(1024)S(1)} %get-tuple-element.122, ...), channel_id=1, replica_groups=mesh['member'=4,'tile'=8] {'member'}, use_global_device_ids=true, to_apply=%region_61.62 | all-reduce | flops 3456 | bytes 27648 | tf_op jit(solution)/shard_map/psum | solution.py:208
  254.0 17.6 %collective-permute-done.9 = bf16[384,384]{1,0:T(8,128)(2,1)} collective-permute-done((bf16[384,384]{1,0:T(8,128)(2,1)S(1)}, bf16[384,384]{1,0:T(8,128)(2,1)}, u32[]{:S(2)}, u32[]{:S(2)}) %collective-permute-start.9) | collective-permute-done | bytes 294944 | tf_op jit(solution)/shard_map/ppermute | solution.py:16
  271.6 4.8 %fusion.192 = (bf16[96,384]{1,0:T(8,128)(2,1)S(1)}, bf16[96,384]{1,0:T(8,128)(2,1)S(1)}, bf16[96,384]{1,0:T(8,128)(2,1)S(1)}, bf16[96,384]{1,0:T(8,128)(2,1)S(1)...) fusion(bf16[384,384]{1,0:T(8,128)(2,1)} %copy-done.10, bf16[384,384]{1,0:T(8,128)(2,1)S(1)} %collective-permute-done.11, ...), kind=kLoop, calls=%fused_computation.418 | loop fusion | flops 221184 | bytes 1253382 | tf_op jit(solution)/shard_map/slice | solution.py:58
  276.4 4.9 %fusion.191 = (bf16[96,384]{1,0:T(8,128)(2,1)S(1)}, bf16[96,384]{1,0:T(8,128)(2,1)S(1)}, bf16[96,384]{1,0:T(8,128)(2,1)S(1)}, bf16[96,384]{1,0:T(8,128)(2,1)S(1)...) fusion(bf16[384,384]{1,0:T(8,128)(2,1)S(1)} %collective-permute, ...), kind=kLoop, calls=%fused_computation.417 | loop fusion | flops 221184 | bytes 1548294 | tf_op jit(solution)/shard_map/slice | solution.py:57
  281.4 3.6 fusion.153
  285.1 3.8 fusion.148
  288.8 3.7 fusion.163
  292.5 3.8 fusion.158
  296.4 3.8 select_select_fusion
  300.1 3.8 select_select_fusion.1
  304.0 4.5 maximum_maximum_fusion.2
  308.5 44.8 %all-reduce.7.cloned.1.call-done = (f32[384,1536]{0,1:T(8,128)}, f32[1536,384]{1,0:T(8,128)}, f32[7,7,384]{2,1,0:T(8,128)}) async-done(((f32[384,1536]{0,1:T(8,128)}, f32[1536,384]{1,0:T(8,128)}, f32[7,7,384]{2,1,0:T(8,128)}), (f32[384,1536]{0,1:T(8,128)}, f32[1536,384]{1,0:T(8,128)}, f32[7,7,384]{2,1,0:T(8,128)})) %all-reduce.7.cloned.1.call-update) | async-done | bytes 4793872 | tf_op jit(solution)/shard_map/psum | solution.py:209
  354.0 16.2 %fusion.123 = bf16[1,1,32,32,384]{4,3,2,1,0:T(8,128)(2,1)} fusion(bf16[35,38,384]{2,1,0:T(8,128)(2,1)S(1)} %get-tuple-element.148, f32[384]{0:T(512)} %get-tuple-element.120, f32[384]{0:T(512)} %get-tuple-element.121, f32[384]{0:T(512)} %get-tuple-element.74, f32[384]{0:T(512)} %get-tuple-element.75, f32[384]{0:T(512)} %get-tuple-element.76, ...), kind=kLoop, calls=%fused_computation.259 | loop fusion | flops 65667072 | bytes 35612160 | tf_op jit(solution)/shard_map/reshape | solution.py:231
  370.2 80.7 %all-reduce.9.cloned.1.call-done = (f32[384,1536]{0,1:T(8,128)}, f32[1536,384]{1,0:T(8,128)}, f32[7,7,384]{2,1,0:T(8,128)}) async-done(((f32[384,1536]{0,1:T(8,128)}, f32[1536,384]{1,0:T(8,128)}, f32[7,7,384]{2,1,0:T(8,128)}), (f32[384,1536]{0,1:T(8,128)}, f32[1536,384]{1,0:T(8,128)}, f32[7,7,384]{2,1,0:T(8,128)})) %all-reduce.9.cloned.1.call-update) | async-done | bytes 4793872 | tf_op jit(solution)/shard_map/psum | solution.py:208
  (281 shorter events, 53.3 us)
Async XLA Ops:
  7.2 99.9 %copy-start = (bf16[384,1536]{1,0:T(8,128)(2,1)S(1)}, bf16[384,1536]{1,0:T(8,128)(2,1)}, u32[]{:S(2)}) copy-start(bf16[384,1536]{1,0:T(8,128)(2,1)} %param.19) | copy-start | bytes 3538948
  7.2 15.3 %copy-start.13 = (f32[7,7,384]{2,1,0:T(8,128)S(1)}, f32[7,7,384]{2,1,0:T(8,128)}, u32[]{:S(2)}) copy-start(f32[7,7,384]{2,1,0:T(8,128)} %param.15) | copy-start | bytes 225796
  7.2 346.1 %all-reduce.7.cloned.1.call-start = ((), (), s32[]{:S(2)}) async-start(), calls=%async_computation | async-start | bytes 9609216 | tf_op jit(solution)/shard_map/psum | solution.py:209
  9.6 13.6 %collective-permute-start = (bf16[384,384]{1,0:T(8,128)(2,1)S(1)}, bf16[384,384]{1,0:T(8,128)(2,1)S(1)}, u32[]{:S(2)}, u32[]{:S(2)}) collective-permute-start(bf16[384,384]{1,0:T(8,128)(2,1)S(1)} %pad_maximum_fusion.4), channel_id=1, source_target_pairs={{0,5},{1,6},{2,7},{3,0},{4,1},{5,2},{6,3},{7,4},{8,13},{9,14},{10,... | collective-permute-start | bytes 884744 | tf_op jit(solution)/shard_map/ppermute | solution.py:16
  14.6 18.1 %collective-permute-start.1 = (bf16[384,384]{1,0:T(8,128)(2,1)S(1)}, bf16[384,384]{1,0:T(8,128)(2,1)S(1)}, u32[]{:S(2)}, u32[]{:S(2)}) collective-permute-start(bf16[384,384]{1,0:T(8,128)(2,1)S(1)} %pad_maximum_fusion.4), channel_id=1, source_target_pairs={{0,6},{1,7},{2,0},{3,1},{4,2},{5,3},{6,4},{7,5},{8,14},{9,15},{10,... | collective-permute-start | bytes 884744 | tf_op jit(solution)/shard_map/ppermute | solution.py:16
  15.9 18.8 %collective-permute-start.2 = (bf16[384,384]{1,0:T(8,128)(2,1)S(1)}, bf16[384,384]{1,0:T(8,128)(2,1)S(1)}, u32[]{:S(2)}, u32[]{:S(2)}) collective-permute-start(bf16[384,384]{1,0:T(8,128)(2,1)S(1)} %pad_maximum_fusion.4), channel_id=1, source_target_pairs={{0,7},{1,0},{2,1},{3,2},{4,3},{5,4},{6,5},{7,6},{8,15},{9,8},{10,9... | collective-permute-start | bytes 884744 | tf_op jit(solution)/shard_map/ppermute | solution.py:16
  16.5 36.9 %collective-permute-start.3 = (bf16[384,384]{1,0:T(8,128)(2,1)S(1)}, bf16[384,384]{1,0:T(8,128)(2,1)S(1)}, u32[]{:S(2)}, u32[]{:S(2)}) collective-permute-start(bf16[384,384]{1,0:T(8,128)(2,1)S(1)} %pad_maximum_fusion.4), channel_id=1, source_target_pairs={{0,3},{1,4},{2,5},{3,6},{4,7},{5,0},{6,1},{7,2},{8,11},{9,12},{10,... | collective-permute-start | bytes 884744 | tf_op jit(solution)/shard_map/ppermute | solution.py:16
  18.1 35.3 %collective-permute-start.4 = (bf16[384,384]{1,0:T(8,128)(2,1)S(1)}, bf16[384,384]{1,0:T(8,128)(2,1)S(1)}, u32[]{:S(2)}, u32[]{:S(2)}) collective-permute-start(bf16[384,384]{1,0:T(8,128)(2,1)S(1)} %pad_maximum_fusion.4), channel_id=1, source_target_pairs={{0,2},{1,3},{2,4},{3,5},{4,6},{5,7},{6,0},{7,1},{8,10},{9,11},{10,... | collective-permute-start | bytes 884744 | tf_op jit(solution)/shard_map/ppermute | solution.py:16
  23.2 66.3 %copy-start.14 = (f32[384]{0:T(512)}, f32[384]{0:T(512)S(1)}, u32[]{:S(2)}) copy-start(f32[384]{0:T(512)S(1)} %get-tuple-element.111) | copy-start | bytes 4612
  23.2 66.3 %copy-start.16 = (f32[384]{0:T(512)}, f32[384]{0:T(512)S(1)}, u32[]{:S(2)}) copy-start(f32[384]{0:T(512)S(1)} %get-tuple-element.112) | copy-start | bytes 4612
  23.2 66.3 %copy-start.18 = (f32[384]{0:T(512)}, f32[384]{0:T(512)S(1)}, u32[]{:S(2)}) copy-start(f32[384]{0:T(512)S(1)} %get-tuple-element.113) | copy-start | bytes 4612
  23.2 66.4 %copy-start.20 = (f32[384]{0:T(512)}, f32[384]{0:T(512)S(1)}, u32[]{:S(2)}) copy-start(f32[384]{0:T(512)S(1)} %get-tuple-element.114) | copy-start | bytes 4612
  23.2 30.2 %collective-permute-start.5 = (bf16[384,384]{1,0:T(8,128)(2,1)S(1)}, bf16[384,384]{1,0:T(8,128)(2,1)S(1)}, u32[]{:S(2)}, u32[]{:S(2)}) collective-permute-start(bf16[384,384]{1,0:T(8,128)(2,1)S(1)} %pad_maximum_fusion.4), channel_id=1, source_target_pairs={{0,1},{1,2},{2,3},{3,4},{4,5},{5,6},{6,7},{7,0},{8,9},{9,10},{10,1... | collective-permute-start | bytes 884744 | tf_op jit(solution)/shard_map/ppermute | solution.py:16
  84.5 5.1 %copy-start.4 = (bf16[1,1,32,32,384]{4,3,2,1,0:T(8,128)(2,1)S(1)}, bf16[1,1,32,32,384]{4,3,2,1,0:T(8,128)(2,1)}, u32[]{:S(2)}) copy-start(bf16[1,1,32,32,384]{4,3,2,1,0:T(8,128)(2,1)} %param.12) | copy-start | bytes 2359300
  84.5 5.1 %copy-start.22 = (f32[384]{0:T(512)S(1)}, f32[384]{0:T(512)}, u32[]{:S(2)}) copy-start(f32[384]{0:T(512)} %get-tuple-element.115) | copy-start | bytes 4612
  84.5 5.1 %copy-start.24 = (f32[384]{0:T(512)S(1)}, f32[384]{0:T(512)}, u32[]{:S(2)}) copy-start(f32[384]{0:T(512)} %get-tuple-element.116) | copy-start | bytes 4612
  84.5 5.1 %copy-start.26 = (f32[384]{0:T(512)S(1)}, f32[384]{0:T(512)}, u32[]{:S(2)}) copy-start(f32[384]{0:T(512)} %get-tuple-element.117) | copy-start | bytes 4612
  84.5 5.1 %copy-start.27 = (f32[384]{0:T(512)S(1)}, f32[384]{0:T(512)}, u32[]{:S(2)}) copy-start(f32[384]{0:T(512)} %get-tuple-element.118) | copy-start | bytes 4612
  113.6 6.3 %copy-start.3 = (f32[32,32,384]{2,1,0:T(8,128)S(1)}, f32[32,32,384]{2,1,0:T(8,128)}, u32[]{:S(2)}) copy-start(f32[32,32,384]{2,1,0:T(8,128)} %get-tuple-element.142) | copy-start | bytes 4718596
  113.6 6.3 %copy-start.62 = (f32[384]{0:T(512)S(1)}, f32[384]{0:T(512)}, u32[]{:S(2)}) copy-start(f32[384]{0:T(512)} %param.17) | copy-start | bytes 4612
  143.1 307.8 %all-reduce.9.cloned.1.call-start = ((), (), s32[]{:S(2)}) async-start(), calls=%async_computation.1 | async-start | bytes 9609216 | tf_op jit(solution)/shard_map/psum | solution.py:208
  144.0 132.4 %copy-start.6 = (bf16[32,32,384]{2,1,0:T(8,128)(2,1)}, bf16[32,32,384]{2,1,0:T(8,128)(2,1)S(1)}, u32[]{:S(2)}) copy-start(bf16[32,32,384]{2,1,0:T(8,128)(2,1)S(1)} %convert_element_type.446) | copy-start | bytes 2359300
  144.1 9.0 %copy-start.63 = (f32[1536]{0:T(1024)S(1)}, f32[1536]{0:T(1024)}, u32[]{:S(2)}) copy-start(f32[1536]{0:T(1024)} %get-tuple-element.244) | copy-start | bytes 18436
  144.1 9.0 %copy-start.66 = (f32[384]{0:T(512)S(1)}, f32[384]{0:T(512)}, u32[]{:S(2)}) copy-start(f32[384]{0:T(512)} %get-tuple-element.145) | copy-start | bytes 4612
  144.1 9.0 %copy-start.67 = (f32[384]{0:T(512)S(1)}, f32[384]{0:T(512)}, u32[]{:S(2)}) copy-start(f32[384]{0:T(512)} %get-tuple-element.7) | copy-start | bytes 4612
  144.1 9.0 %copy-start.68 = (f32[384]{0:T(512)S(1)}, f32[384]{0:T(512)}, u32[]{:S(2)}) copy-start(f32[384]{0:T(512)} %get-tuple-element.61) | copy-start | bytes 4612
  144.4 107.6 %collective-permute-start.10 = (bf16[384,384]{1,0:T(8,128)(2,1)S(1)}, bf16[384,384]{1,0:T(8,128)(2,1)}, u32[]{:S(2)}, u32[]{:S(2)}) collective-permute-start(bf16[384,384]{1,0:T(8,128)(2,1)S(1)} %pad_maximum_fusion.5), channel_id=1, source_target_pairs={{0,2},{1,3},{2,4},{3,5},{4,6},{5,7},{6,0},{7,1},{8,10},{9,11},{10,... | collective-permute-start | bytes 884744 | tf_op jit(solution)/shard_map/ppermute | solution.py:16
  145.7 107.6 %collective-permute-start.11 = (bf16[384,384]{1,0:T(8,128)(2,1)S(1)}, bf16[384,384]{1,0:T(8,128)(2,1)S(1)}, u32[]{:S(2)}, u32[]{:S(2)}) collective-permute-start(bf16[384,384]{1,0:T(8,128)(2,1)S(1)} %pad_maximum_fusion.5), channel_id=1, source_target_pairs={{0,1},{1,2},{2,3},{3,4},{4,5},{5,6},{6,7},{7,0},{8,9},{9,10},{10,1... | collective-permute-start | bytes 884744 | tf_op jit(solution)/shard_map/ppermute | solution.py:16
  147.4 105.8 %collective-permute-start.6 = (bf16[384,384]{1,0:T(8,128)(2,1)S(1)}, bf16[384,384]{1,0:T(8,128)(2,1)S(1)}, u32[]{:S(2)}, u32[]{:S(2)}) collective-permute-start(bf16[384,384]{1,0:T(8,128)(2,1)S(1)} %pad_maximum_fusion.5), channel_id=1, source_target_pairs={{0,5},{1,6},{2,7},{3,0},{4,1},{5,2},{6,3},{7,4},{8,13},{9,14},{10,... | collective-permute-start | bytes 884744 | tf_op jit(solution)/shard_map/ppermute | solution.py:16
  150.0 103.2 %collective-permute-start.7 = (bf16[384,384]{1,0:T(8,128)(2,1)S(1)}, bf16[384,384]{1,0:T(8,128)(2,1)S(1)}, u32[]{:S(2)}, u32[]{:S(2)}) collective-permute-start(bf16[384,384]{1,0:T(8,128)(2,1)S(1)} %pad_maximum_fusion.5), channel_id=1, source_target_pairs={{0,6},{1,7},{2,0},{3,1},{4,2},{5,3},{6,4},{7,5},{8,14},{9,15},{10,... | collective-permute-start | bytes 884744 | tf_op jit(solution)/shard_map/ppermute | solution.py:16
  153.1 100.2 %collective-permute-start.8 = (bf16[384,384]{1,0:T(8,128)(2,1)S(1)}, bf16[384,384]{1,0:T(8,128)(2,1)}, u32[]{:S(2)}, u32[]{:S(2)}) collective-permute-start(bf16[384,384]{1,0:T(8,128)(2,1)S(1)} %pad_maximum_fusion.5), channel_id=1, source_target_pairs={{0,7},{1,0},{2,1},{3,2},{4,3},{5,4},{6,5},{7,6},{8,15},{9,8},{10,9... | collective-permute-start | bytes 884744 | tf_op jit(solution)/shard_map/ppermute | solution.py:16
  252.0 19.6 %collective-permute-start.9 = (bf16[384,384]{1,0:T(8,128)(2,1)S(1)}, bf16[384,384]{1,0:T(8,128)(2,1)}, u32[]{:S(2)}, u32[]{:S(2)}) collective-permute-start(bf16[384,384]{1,0:T(8,128)(2,1)S(1)} %pad_maximum_fusion.5), channel_id=1, source_target_pairs={{0,3},{1,4},{2,5},{3,6},{4,7},{5,0},{6,1},{7,2},{8,11},{9,12},{10,... | collective-permute-start | bytes 884744 | tf_op jit(solution)/shard_map/ppermute | solution.py:16
  (54 other events, 208.7 us)
Sparse Core Ops, SparseCore 0:
  143.3 209.9 all-reduce.6
  356.0 94.8 all-reduce.8
